TPU v7x, 256 devices: a whole 4x4x8 slice. The times are simulated.
256 devices in a mesh: dp: 16 (over x, y), head: 16 (over z, core).
Axes of the slice: x: 4, y: 4, z: 8, core: 2. Of those that a mesh axis runs over, the one named last changes fastest.
Arguments:
- query: bfloat16 [32768, 12288], P(('dp', 'head')), may hold values from -160 to 160
- latent: bfloat16 [32768, 576], P(('dp', 'head')), may hold values from -6 to 6
- d_attn: bfloat16 [32768, 8192], P(('dp', 'head')), may hold values from -6 to 6
- w_kv: bfloat16 [512, 16384], P('dp', 'head'), may hold values from -0.25 to 0.25
- doc_lengths: int32 [16, 10], P('dp'), may hold values from 1 to 384, 2048 in all within a row
Outputs:
- d_query: bfloat16 [32768, 12288], P(('dp', 'head'))
- d_latent: float32 [32768, 576], P(('dp', 'head'))
- d_w_kv: float32 [512, 16384], P('dp', 'head')
Inputs may be any that keep to these rules, and one draw needn't show every extreme that they name: `doc_lengths`: row g lists the lengths of the 10 documents of data group g; they sum to 2048, and the longest of each row is exactly 384.
All inputs are finite; a program needn't handle non-finite values.
Results may differ from a plain program's by a relative error of at most 0.025.
Values may be sent and summed in bfloat16 or wider, within the bound.
No kernel may reach another device: no remote copies, remote signals or barrier semaphores. Data moves between devices by JAX's collectives and lax.ppermute only.
A program may use at most 128 MiB of HBM per device.

v0:
```python
import math
import jax
import jax.numpy as jnp
from jax import lax
from jax.sharding import PartitionSpec as P

NOPE = 128
ROPE = 64
VDIM = 128
KV_RANK = 512
DOC_MAX = 384
QB = 128
masked_score = -1e30


def document_index(lengths_row, count):
    ends = jnp.cumsum(lengths_row)
    positions = jnp.arange(count, dtype=jnp.int32)
    return jnp.sum((positions[:, None] >= ends[None, :]).astype(jnp.int32), axis=1)


def attend_backward(queries, keys_padded, values_padded, grads_out, doc_padded, block, window):
    seq_len = queries.shape[0]
    reach = window - block
    scale = 1.0 / math.sqrt(queries.shape[2])
    blocks = seq_len // block

    def one_block(carry, index):
        grad_keys, grad_values = carry
        first = index * block
        query_rows = lax.dynamic_slice_in_dim(queries, first, block, 0)
        key_rows = lax.dynamic_slice_in_dim(keys_padded, first, window, 0)
        value_rows = lax.dynamic_slice_in_dim(values_padded, first, window, 0)
        out_rows = lax.dynamic_slice_in_dim(grads_out, first, block, 0)
        query_doc = lax.dynamic_slice_in_dim(doc_padded, first + reach, block, 0)
        key_doc = lax.dynamic_slice_in_dim(doc_padded, first, window, 0)
        query_pos = jnp.arange(block, dtype=jnp.int32) + reach
        key_pos = jnp.arange(window, dtype=jnp.int32)
        allowed = (key_pos[None, :] <= query_pos[:, None]) & (
            key_doc[None, :] == query_doc[:, None]
        )
        scores = (
            jnp.einsum("qhd,khd->hqk", query_rows, key_rows, preferred_element_type=jnp.float32)
            * scale
        )
        scores = jnp.where(allowed[None], scores, masked_score)
        top = jnp.max(scores, axis=2, keepdims=True)
        weights = jnp.exp(scores - top)
        probs = weights / jnp.sum(weights, axis=2, keepdims=True)
        probs_low = probs.astype(jnp.bfloat16)
        attn_out = jnp.einsum(
            "hqk,khd->qhd", probs_low, value_rows, preferred_element_type=jnp.float32
        )
        delta = jnp.sum(out_rows.astype(jnp.float32) * attn_out, axis=2)
        dprob = jnp.einsum("qhd,khd->hqk", out_rows, value_rows, preferred_element_type=jnp.float32)
        dscore_low = (probs * (dprob - jnp.transpose(delta)[:, :, None])).astype(jnp.bfloat16)
        grad_query = (
            jnp.einsum("hqk,khd->qhd", dscore_low, key_rows, preferred_element_type=jnp.float32)
            * scale
        )
        grad_key_rows = (
            jnp.einsum("hqk,qhd->khd", dscore_low, query_rows, preferred_element_type=jnp.float32)
            * scale
        )
        grad_value_rows = jnp.einsum(
            "hqk,qhd->khd", probs_low, out_rows, preferred_element_type=jnp.float32
        )
        grad_keys = lax.dynamic_update_slice_in_dim(
            grad_keys,
            lax.dynamic_slice_in_dim(grad_keys, first, window, 0) + grad_key_rows,
            first,
            0,
        )
        grad_values = lax.dynamic_update_slice_in_dim(
            grad_values,
            lax.dynamic_slice_in_dim(grad_values, first, window, 0) + grad_value_rows,
            first,
            0,
        )
        return ((grad_keys, grad_values), grad_query.astype(jnp.bfloat16))

    start_keys = jnp.zeros(keys_padded.shape, jnp.float32)
    start_values = jnp.zeros(values_padded.shape, jnp.float32)
    (grad_keys, grad_values), grad_queries = lax.scan(
        one_block, (start_keys, start_values), jnp.arange(blocks, dtype=jnp.int32)
    )
    grad_queries = grad_queries.reshape(seq_len, queries.shape[1] * queries.shape[2])
    return (grad_keys[reach:], grad_values[reach:], grad_queries)


def local(query, latent, d_attn, w_kv, doc_lengths):
    group_size = lax.axis_size("head")
    own_tokens = query.shape[0]
    seq_len = own_tokens * group_size
    head_count = w_kv.shape[1] // (NOPE + VDIM)
    queries, grads_out = (
        lax.all_to_all(query, "head", split_axis=1, concat_axis=0, tiled=True),
        lax.all_to_all(d_attn, "head", split_axis=1, concat_axis=0, tiled=True),
    )
    latents = lax.all_gather(latent, "head", axis=0, tiled=True)
    compressed = latents[:, :KV_RANK]
    whole_weight = lax.all_gather(w_kv, "dp", axis=0, tiled=True)
    kv_up = jnp.dot(compressed, whole_weight, preferred_element_type=jnp.float32)
    kv_up = kv_up.astype(jnp.bfloat16).reshape(seq_len, head_count, NOPE + VDIM)
    rotary = jnp.broadcast_to(latents[:, None, KV_RANK:], (seq_len, head_count, ROPE))
    keys = jnp.concatenate([kv_up[:, :, :NOPE], rotary], axis=2)
    keys_padded = jnp.concatenate(
        [jnp.zeros((DOC_MAX, head_count, NOPE + ROPE), jnp.bfloat16), keys], axis=0
    )
    values_padded = jnp.concatenate(
        [jnp.zeros((DOC_MAX, head_count, VDIM), jnp.bfloat16), kv_up[:, :, NOPE:]], axis=0
    )
    doc_ids = document_index(doc_lengths[0], seq_len)
    doc_padded = jnp.concatenate([jnp.full((DOC_MAX,), -1, jnp.int32), doc_ids])
    grad_keys, grad_values, grad_queries = attend_backward(
        queries.reshape(seq_len, head_count, NOPE + ROPE),
        keys_padded,
        values_padded,
        grads_out.reshape(seq_len, head_count, VDIM),
        doc_padded,
        QB,
        DOC_MAX + QB,
    )
    returned = lax.all_to_all(grad_queries, "head", split_axis=0, concat_axis=1, tiled=True)
    grad_kv = jnp.concatenate([grad_keys[:, :, :NOPE], grad_values], axis=2).astype(jnp.bfloat16)
    grad_kv = grad_kv.reshape(seq_len, head_count * (NOPE + VDIM))
    grad_weight = lax.psum_scatter(
        lax.dot_general(
            compressed, grad_kv, (((0,), (0,)), ((), ())), preferred_element_type=jnp.float32
        ).astype(jnp.bfloat16),
        "dp",
        scatter_dimension=0,
        tiled=True,
    ).astype(jnp.float32)
    grad_compressed = lax.dot_general(
        grad_kv, whole_weight, (((1,), (1,)), ((), ())), preferred_element_type=jnp.float32
    )
    head_terms = jnp.concatenate([grad_compressed, jnp.sum(grad_keys[:, :, NOPE:], axis=1)], axis=1)
    summed = lax.psum(head_terms.astype(jnp.bfloat16), "head").astype(jnp.float32)
    grad_latent = lax.dynamic_slice_in_dim(
        summed, lax.axis_index("head") * own_tokens, own_tokens, 0
    )
    return (returned, grad_latent, grad_weight)


def solution(mesh):
    placed = (
        P(("dp", "head"), None),
        P(("dp", "head"), None),
        P(("dp", "head"), None),
        P("dp", "head"),
        P("dp", None),
    )
    return jax.shard_map(
        local,
        mesh=mesh,
        in_specs=placed,
        out_specs=(P(("dp", "head"), None), P(("dp", "head"), None), P("dp", "head")),
        check_vma=False,
    )
```

profile of v0, /device:TPU:2, one launch (start us, length us, event | category | flops | bytes accessed | tf_op | source)
XLA Modules:
  0.0 728.3 jit_solution(18205139117940249030)
XLA Ops:
  7.2 4.1 copy.52
  11.2 8.6 %all-to-all-start.1 = ((bf16[128,16,512]{0,2,1:T(8,128)(2,1)}), bf16[128,16,512]{0,2,1:T(8,128)(2,1)S(1)}, u32[]{:S(2)}, u32[]{:S(2)}) async-start(bf16[128,16,512]{0,2,1:T(8,128)(2,1)} %bitcast.74), calls=%async_computation.1 | async-start | bytes 4194304 | tf_op jit(solution)/shard_map/all_to_all | solution.py:98
  21.3 4.6 copy.50
  25.9 43.1 %all-to-all-done.1 = bf16[128,16,512]{0,2,1:T(8,128)(2,1)S(1)} async-done(((bf16[128,16,512]{0,2,1:T(8,128)(2,1)}), bf16[128,16,512]{0,2,1:T(8,128)(2,1)S(1)}, u32[]{:S(2)}, u32[]{:S(2)}) %all-to-all-start.1) | async-done | bytes 2097184 | tf_op jit(solution)/shard_map/all_to_all | solution.py:98
  70.4 4.7 all-to-all-start
  75.4 4.3 copy.53
  79.7 4.2 reshape.117
  83.9 74.2 %all-gather.3.cloned.1.call-done = bf16[2048,576]{0,1:T(8,128)(2,1)} async-done(((bf16[128,576]{0,1:T(8,128)(2,1)}), bf16[2048,576]{0,1:T(8,128)(2,1)}) %all-gather.3.cloned.1.call-update) | async-done | bytes 2359312 | tf_op jit(solution)/shard_map/all_gather | solution.py:100
  158.1 4.2 convolution_convert_fusion
  162.4 2.6 fusion.75
  165.0 4.0 copy.66
  168.9 3.4 concatenate.23
  174.4 3.7 copy.51
  178.1 5.8 reshape.113
  183.9 3.5 broadcast_in_dim.54
  187.4 2.6 broadcast_in_dim.55
  190.0 266.0 %while.16 = (s32[]{:T(128)}, f32[2432,4,192]{0,2,1:T(8,128)}, f32[2432,4,128]{0,2,1:T(8,128)}, bf16[16,128,4,192]{1,3,2,0:T(8,128)(2,1)}, s32[16]{0:T(128)S(1)},...) while((s32[]{:T(128)}, f32[2432,4,192]{0,2,1:T(8,128)}, ...), condition=%wide.region_6.7_spmd, body=%wide.region_2.6_spmd.sunk | while | flops 711002240 | bytes 15294786 | solution.py:84
  198.0 3.1 fusion.127
  201.1 3.3 fusion.128
  214.7 3.2 fusion.127
  217.8 3.3 fusion.128
  231.3 3.1 fusion.127
  234.4 3.3 fusion.128
  247.9 3.1 fusion.127
  251.0 3.3 fusion.128
  264.5 3.1 fusion.127
  267.7 3.3 fusion.128
  281.2 3.1 fusion.127
  284.3 3.3 fusion.128
  297.8 3.1 fusion.127
  300.9 3.3 fusion.128
  304.2 2.2 fusion.129
  314.4 3.1 fusion.127
  317.5 3.3 fusion.128
  331.0 3.1 fusion.127
  334.1 3.3 fusion.128
  347.6 3.1 fusion.127
  350.7 3.3 fusion.128
  354.0 2.2 fusion.129
  364.3 3.1 fusion.127
  367.3 3.3 fusion.128
  380.8 3.1 fusion.127
  384.0 3.3 fusion.128
  397.5 3.1 fusion.127
  400.6 3.3 fusion.128
  414.1 3.1 fusion.127
  417.2 3.3 fusion.128
  420.6 2.2 fusion.129
  430.8 3.1 fusion.127
  433.8 3.3 fusion.128
  447.4 3.1 fusion.127
  450.5 3.3 fusion.128
  453.8 2.2 fusion.129
  455.9 4.7 copy.56
  460.6 6.1 all-to-all-start.2
  466.9 2.5 slice.51
  469.4 2.5 slice.50
  475.0 2.3 convolution_convert_fusion.1
  479.1 6.3 fusion.67
  485.4 2.3 copy.63
  487.7 142.7 %all-reduce.5.cloned.1.call-done = bf16[2048,576]{0,1:T(8,128)(2,1)} async-done(((bf16[2048,576]{0,1:T(8,128)(2,1)}), bf16[2048,576]{0,1:T(8,128)(2,1)}) %all-reduce.5.cloned.1.call-update) | async-done | bytes 2359312 | tf_op jit(solution)/shard_map/psum | solution.py:139
  632.0 80.5 %reduce-scatter.4.cloned.1.call-done = bf16[32,1024]{1,0:T(8,128)(2,1)} async-done(((bf16[512,1024]{1,0:T(8,128)(2,1)}), bf16[32,1024]{1,0:T(8,128)(2,1)}) %reduce-scatter.4.cloned.1.call-update) | async-done | bytes 65552
  714.3 2.8 copy.57
  717.1 4.6 copy.58
  (208 shorter events, 157.3 us)
Async XLA Ops:
  11.2 57.8 %all-to-all-start.1 = ((bf16[128,16,512]{0,2,1:T(8,128)(2,1)}), bf16[128,16,512]{0,2,1:T(8,128)(2,1)S(1)}, u32[]{:S(2)}, u32[]{:S(2)}) async-start(bf16[128,16,512]{0,2,1:T(8,128)(2,1)} %bitcast.74), calls=%async_computation.1 | async-start | bytes 4194304 | tf_op jit(solution)/shard_map/all_to_all | solution.py:98
  19.8 64.1 %all-gather.5.cloned.1.call-start = ((), (), s32[]{:S(2)}) async-start(), calls=%async_computation.5 | async-start | bytes 1114112 | tf_op jit(solution)/shard_map/all_gather | solution.py:102
  20.6 137.6 %all-gather.3.cloned.1.call-start = ((), (), s32[]{:S(2)}) async-start(), calls=%async_computation.4 | async-start | bytes 2506752 | tf_op jit(solution)/shard_map/all_gather | solution.py:100
  69.0 1.4 copy-start
  69.0 6.0 copy-start.4
  70.4 104.0 %all-to-all-start = ((bf16[128,16,768]{0,2,1:T(8,128)(2,1)}), bf16[128,16,768]{0,2,1:T(8,128)(2,1)S(1)}, u32[]{:S(2)}, u32[]{:S(2)}) async-start(bf16[128,16,768]{0,2,1:T(8,128)(2,1)} %bitcast.7), calls=%async_computation | async-start | bytes 6291456 | tf_op jit(solution)/shard_map/all_to_all | solution.py:97
  168.9 3.4 slice-start
  168.9 3.5 copy-start.1
  460.6 253.7 %all-to-all-start.2 = ((bf16[16,128,768]{2,1,0:T(8,128)(2,1)}), bf16[16,128,768]{2,1,0:T(8,128)(2,1)S(1)}, u32[]{:S(2)}, u32[]{:S(2)}) async-start(bf16[16,128,768]{2,1,0:T(8,128)(2,1)} %copy.56), calls=%async_computation.2 | async-start | bytes 6291456 | tf_op jit(solution)/shard_map/all_to_all | solution.py:124
  466.7 163.7 %all-reduce.5.cloned.1.call-start = ((), (), s32[]{:S(2)}) async-start(), calls=%async_computation.6 | async-start | bytes 4718592 | tf_op jit(solution)/shard_map/psum | solution.py:139
  473.7 1.2 copy-start.3
  474.3 3.0 copy-start.2
  479.0 233.5 %reduce-scatter.4.cloned.1.call-start = ((), (), s32[]{:S(2)}) async-start(), calls=%async_computation.7 | async-start | bytes 1114112
Sparse Core Ops, SparseCore 0:
  23.1 48.6 all-gather.4
  73.5 84.6 all-gather.2
  479.2 151.1 all-reduce.4
  633.7 78.7 reduce-scatter.3
where the time goes:
time: 733 us; the launch traced here: 728 us
  waiting for transfers between devices  342 us (47%)
  matrix products  237 us (32%)
  local copies, waits for them, and re-layouts  94.5 us (13%)
  starting transfers between devices  19.7 us (3%)
  between operations  13.9 us (2%)
  loops' own time  11.1 us (2%)
  other arithmetic  10.1 us (1%)
    psum x1, waiting for transfers between devices, local(): lax.psum(head_terms.astype(jnp.bfloat16), 'head').astype(jnp.float32)  143 us
    unnamed x5, waiting for transfers between devices  81.9 us
    all_gather x1, waiting for transfers between devices, local(): latents = lax.all_gather(latent, 'head', axis=0, tiled=True)  74.2 us
    dot_general x16, matrix products, one_block(): jnp.einsum('hqk,qhd->khd', probs_low, out_rows, preferred_element_type=jn...  52.8 us
    dot_general x16, matrix products, one_block(): jnp.einsum('hqk,qhd->khd', dscore_low, query_rows, preferred_element_type...  49.7 us
    all_to_all x1, waiting for transfers between devices, local(): lax.all_to_all(d_attn, 'head', split_axis=1, concat_axis=0, tiled=True)  43.1 us
    dot_general x16, matrix products, one_block(): jnp.einsum('hqk,khd->qhd', dscore_low, key_rows, preferred_element_type=j...  34.8 us
    dot_general x16, matrix products, one_block(): jnp.einsum('hqk,khd->qhd', probs_low, value_rows, preferred_element_type=...  34.8 us
  transfers between devices with their start and end apart: 7, of which 4 were waited for; matrix products, arithmetic and copies ran while one was open for 7% of the time, Pallas kernels for 0%

commit v1 on v0

--- a/solution.py
+++ b/solution.py
@@ -136,7 +136,9 @@
         grad_kv, whole_weight, (((1,), (1,)), ((), ())), preferred_element_type=jnp.float32
     )
     head_terms = jnp.concatenate([grad_compressed, jnp.sum(grad_keys[:, :, NOPE:], axis=1)], axis=1)
-    summed = lax.psum(head_terms.astype(jnp.bfloat16), "head").astype(jnp.float32)
+    summed = jnp.sum(lax.all_gather(head_terms.astype(jnp.bfloat16), "head"), axis=0).astype(
+        jnp.float32
+    )
     grad_latent = lax.dynamic_slice_in_dim(
         summed, lax.axis_index("head") * own_tokens, own_tokens, 0
     )

time: 733 us -> 768 us (1.048)
  waiting for transfers between devices: 342 us -> 365 us
  other arithmetic: 10.1 us -> 22.3 us
    all_gather x0 -> x1, waiting for transfers between devices: none -> 177 us  [local(): lax.all_gather(head_terms.astype(jnp.bfloat16), 'head')]
    psum x1 -> x0, waiting for transfers between devices: 143 us -> none  [local(): lax.psum(head_terms.astype(jnp.bfloat16), 'head').astype(jnp.float32)]
    unnamed x5, waiting for transfers between devices: 81.9 us -> 61.8 us
    reduce_sum x0 -> x1, other arithmetic: none -> 13 us  [local(): jnp.sum(lax.all_gather(head_terms.astype(jnp.bfloat16), 'head'), axis=0)]
    all_to_all x1, waiting for transfers between devices: 0.01 us -> 9.61 us  [local(): lax.all_to_all(grad_queries, 'head', split_axis=0, concat_axis=1, tiled=T...]
    unnamed x17 -> x19, local copies, waits for them, and re-layouts: 23.4 us -> 24 us
  transfers between devices with their start and end apart: 7 -> 7, of which waited for: 4 -> 5; matrix products, arithmetic and copies ran while one was open for 7% -> 7% of each run, Pallas kernels for 0% -> 0%
where the time goes in v1:
time: 768 us; the launch traced here: 762 us
  waiting for transfers between devices  365 us (48%)
  matrix products  235 us (31%)
  local copies, waits for them, and re-layouts  95.2 us (12%)
  other arithmetic  22.3 us (3%)
  starting transfers between devices  19.5 us (3%)
  between operations  13.9 us (2%)
  loops' own time  11.1 us (1%)
    all_gather x1, waiting for transfers between devices, local(): lax.all_gather(head_terms.astype(jnp.bfloat16), 'head')  177 us
    all_gather x1, waiting for transfers between devices, local(): latents = lax.all_gather(latent, 'head', axis=0, tiled=True)  74.2 us
    unnamed x5, waiting for transfers between devices  61.8 us
    dot_general x16, matrix products, one_block(): jnp.einsum('hqk,qhd->khd', probs_low, out_rows, preferred_element_type=jn...  52.8 us
    dot_general x16, matrix products, one_block(): jnp.einsum('hqk,qhd->khd', dscore_low, query_rows, preferred_element_type...  49.5 us
    all_to_all x1, waiting for transfers between devices, local(): lax.all_to_all(d_attn, 'head', split_axis=1, concat_axis=0, tiled=True)  43.1 us
    dot_general x16, matrix products, one_block(): jnp.einsum('hqk,khd->qhd', dscore_low, key_rows, preferred_element_type=j...  35 us
    dot_general x16, matrix products, one_block(): jnp.einsum('hqk,khd->qhd', probs_low, value_rows, preferred_element_type=...  34.7 us
  transfers between devices with their start and end apart: 7, of which 5 were waited for; matrix products, arithmetic and copies ran while one was open for 7% of the time, Pallas kernels for 0%

profile of v1, /device:TPU:2, one launch (start us, length us, event | category | flops | bytes accessed | tf_op | source)
XLA Modules:
  0.0 762.4 jit_solution(7429441355461717063)
XLA Ops:
  7.2 4.1 copy.52
  11.2 8.6 %all-to-all-start.1 = ((bf16[128,16,512]{0,2,1:T(8,128)(2,1)}), bf16[128,16,512]{0,2,1:T(8,128)(2,1)S(1)}, u32[]{:S(2)}, u32[]{:S(2)}) async-start(bf16[128,16,512]{0,2,1:T(8,128)(2,1)} %bitcast.79), calls=%async_computation.1 | async-start | bytes 4194304 | tf_op jit(solution)/shard_map/all_to_all | solution.py:98
  21.3 4.6 copy.50
  25.9 43.1 %all-to-all-done.1 = bf16[128,16,512]{0,2,1:T(8,128)(2,1)S(1)} async-done(((bf16[128,16,512]{0,2,1:T(8,128)(2,1)}), bf16[128,16,512]{0,2,1:T(8,128)(2,1)S(1)}, u32[]{:S(2)}, u32[]{:S(2)}) %all-to-all-start.1) | async-done | bytes 2097184 | tf_op jit(solution)/shard_map/all_to_all | solution.py:98
  70.4 4.7 all-to-all-start
  75.4 4.3 copy.53
  79.8 4.2 reshape.148
  84.0 74.2 %all-gather.4.cloned.1.call-done = bf16[2048,576]{0,1:T(8,128)(2,1)} async-done(((bf16[128,576]{0,1:T(8,128)(2,1)}), bf16[2048,576]{0,1:T(8,128)(2,1)}) %all-gather.4.cloned.1.call-update) | async-done | bytes 2359312 | tf_op jit(solution)/shard_map/all_gather | solution.py:100
  158.1 4.2 convolution_convert_fusion
  162.4 2.6 fusion.76
  164.9 4.0 copy.66
  168.9 3.4 concatenate.34
  174.4 3.7 copy.51
  178.1 5.8 reshape.144
  183.9 2.6 broadcast_in_dim.55
  186.5 3.5 broadcast_in_dim.54
  189.9 265.8 %while.16 = (s32[]{:T(128)}, f32[2432,4,192]{0,2,1:T(8,128)}, f32[2432,4,128]{0,2,1:T(8,128)}, bf16[16,128,4,192]{1,3,2,0:T(8,128)(2,1)}, s32[16]{0:T(128)S(1)},...) while((s32[]{:T(128)}, f32[2432,4,192]{0,2,1:T(8,128)}, ...), condition=%wide.region_6.7_spmd, body=%wide.region_2.6_spmd.sunk | while | flops 711002240 | bytes 15294286 | solution.py:84
  200.2 3.3 fusion.129
  203.5 3.1 fusion.128
  214.6 2.2 fusion.130
  216.8 3.3 fusion.129
  220.1 3.1 fusion.128
  231.3 2.2 fusion.130
  233.5 3.3 fusion.129
  236.8 3.1 fusion.128
  250.1 3.3 fusion.129
  253.4 3.1 fusion.128
  266.7 3.3 fusion.129
  270.0 3.1 fusion.128
  283.3 3.3 fusion.129
  286.6 3.1 fusion.128
  299.9 3.3 fusion.129
  303.2 3.1 fusion.128
  316.5 3.3 fusion.129
  319.8 3.1 fusion.128
  333.1 3.3 fusion.129
  336.4 3.1 fusion.128
  349.7 3.3 fusion.129
  353.0 3.1 fusion.128
  366.3 3.3 fusion.129
  369.6 3.1 fusion.128
  382.9 3.3 fusion.129
  386.2 3.1 fusion.128
  399.5 3.3 fusion.129
  402.8 3.1 fusion.128
  413.9 2.2 fusion.130
  416.1 3.3 fusion.129
  419.4 3.1 fusion.128
  432.7 3.3 fusion.129
  436.0 3.1 fusion.128
  449.3 3.3 fusion.129
  452.6 3.1 fusion.128
  455.7 2.5 slice.51
  458.2 2.5 slice.50
  463.4 2.4 fusion.68
  469.0 4.5 fusion.61
  475.3 4.7 copy.56
  480.0 6.1 all-to-all-start.2
  486.1 60.4 %reduce-scatter.4.cloned.1.call-done = bf16[32,1024]{1,0:T(8,128)(2,1)} async-done(((bf16[512,1024]{1,0:T(8,128)(2,1)}), bf16[32,1024]{1,0:T(8,128)(2,1)}) %reduce-scatter.4.cloned.1.call-update) | async-done | bytes 65552
  548.3 9.6 %all-to-all-done.2 = bf16[16,128,768]{2,1,0:T(8,128)(2,1)S(1)} async-done(((bf16[16,128,768]{2,1,0:T(8,128)(2,1)}), bf16[16,128,768]{2,1,0:T(8,128)(2,1)S(1)}, u32[]{:S(2)}, u32[]{:S(2)}) %all-to-all-start.2) | async-done | bytes 3145760 | tf_op jit(solution)/shard_map/all_to_all | solution.py:124
  557.9 2.8 copy.57
  560.7 4.7 copy.58
  565.4 176.6 %all-gather.8.cloned.1.call-done = bf16[16,2048,576]{1,2,0:T(8,128)(2,1)} async-done(((bf16[1,2048,576]{1,2,0:T(8,128)(2,1)}), bf16[16,2048,576]{1,2,0:T(8,128)(2,1)}) %all-gather.8.cloned.1.call-update) | async-done | bytes 37748752 | tf_op jit(solution)/shard_map/all_gather | solution.py:139
  742.0 13.0 %reduce_sum.56 = bf16[2048,576]{0,1:T(8,128)(2,1)S(1)} reduce(bf16[16,2048,576]{1,2,0:T(8,128)(2,1)} %all-gather.8.cloned.1.call-done, bf16[]{:T(256)} %constant.84.clone.1), dimensions={0}, to_apply=%region_8.9 | reduce | flops 17694720 | bytes 40108032 | tf_op jit(solution)/shard_map/reduce_sum | solution.py:139
  (211 shorter events, 161.2 us)
Async XLA Ops:
  11.2 57.8 %all-to-all-start.1 = ((bf16[128,16,512]{0,2,1:T(8,128)(2,1)}), bf16[128,16,512]{0,2,1:T(8,128)(2,1)S(1)}, u32[]{:S(2)}, u32[]{:S(2)}) async-start(bf16[128,16,512]{0,2,1:T(8,128)(2,1)} %bitcast.79), calls=%async_computation.1 | async-start | bytes 4194304 | tf_op jit(solution)/shard_map/all_to_all | solution.py:98
  19.8 64.1 %all-gather.6.cloned.1.call-start = ((), (), s32[]{:S(2)}) async-start(), calls=%async_computation.5 | async-start | bytes 1114112 | tf_op jit(solution)/shard_map/all_gather | solution.py:102
  20.6 137.6 %all-gather.4.cloned.1.call-start = ((), (), s32[]{:S(2)}) async-start(), calls=%async_computation.4 | async-start | bytes 2506752 | tf_op jit(solution)/shard_map/all_gather | solution.py:100
  69.0 1.4 copy-start
  69.0 6.1 copy-start.5
  70.4 104.0 %all-to-all-start = ((bf16[128,16,768]{0,2,1:T(8,128)(2,1)}), bf16[128,16,768]{0,2,1:T(8,128)(2,1)S(1)}, u32[]{:S(2)}, u32[]{:S(2)}) async-start(bf16[128,16,768]{0,2,1:T(8,128)(2,1)} %bitcast.7), calls=%async_computation | async-start | bytes 6291456 | tf_op jit(solution)/shard_map/all_to_all | solution.py:97
  75.1 471.4 %reduce-scatter.4.cloned.1.call-start = ((), (), s32[]{:S(2)}) async-start(), calls=%async_computation.7 | async-start | bytes 1114112
  168.9 3.4 slice-start
  168.9 3.5 copy-start.1
  460.7 2.7 copy-start.3
  461.3 2.1 copy-start.2
  465.8 3.2 copy-start.4
  467.2 274.9 %all-gather.8.cloned.1.call-start = ((), (), s32[]{:S(2)}) async-start(), calls=%async_computation.6 | async-start | bytes 40108032 | tf_op jit(solution)/shard_map/all_gather | solution.py:139
  480.0 77.9 %all-to-all-start.2 = ((bf16[16,128,768]{2,1,0:T(8,128)(2,1)}), bf16[16,128,768]{2,1,0:T(8,128)(2,1)S(1)}, u32[]{:S(2)}, u32[]{:S(2)}) async-start(bf16[16,128,768]{2,1,0:T(8,128)(2,1)} %copy.56), calls=%async_computation.2 | async-start | bytes 6291456 | tf_op jit(solution)/shard_map/all_to_all | solution.py:124
Sparse Core Ops, SparseCore 0:
  23.1 48.6 all-gather.5
  73.5 84.6 all-gather.3
  467.3 79.1 reduce-scatter.3
  548.2 193.8 all-gather.7
